TPU v7x, 128 devices: a whole 4x4x4 slice. The times are simulated.
128 devices in a mesh: shard: 16 (over z, x), context: 4 (over y), tensor: 2 (over core).
Axes of the slice: x: 4, y: 4, z: 4, core: 2. Of those that a mesh axis runs over, the one named last changes fastest.
Arguments:
- inputs: float32 [32, 512, 768], P('shard', 'context'), may hold values from -6 to 6
- segment_ids: int32 [32, 512], P('shard', 'context'), may hold values from 0 to 3, never falling along the last dimension, each value on 1 to 256 neighbouring positions
- projection: bfloat16 [2, 3, 768, 768], P(None, None, 'shard', 'tensor'), may hold values from -1 to 1
- head_bias: bfloat16 [2, 2, 12, 64], P(None, None, 'tensor', 'shard'), may hold values from -3 to 3
- mixing: bfloat16 [2, 768, 768], P(None, 'tensor', 'shard'), may hold values from -0.875 to 0.875
- expansion: bfloat16 [2, 768, 3072], P(None, 'shard', 'tensor'), may hold values from -0.21875 to 0.21875
- hidden_bias: bfloat16 [2, 48, 64], P(None, 'tensor', 'shard'), may hold values from -3 to 3
- contraction: bfloat16 [2, 3072, 768], P(None, 'tensor', 'shard'), may hold values from -0.109375 to 0.109375
- norm_gains: bfloat16 [2, 2, 768], P(None, None, 'shard'), may hold values from 0.3984375 to 1.59375
- offsets: bfloat16 [2, 4, 768], P(None, None, 'shard'), may hold values from -2 to 2
- cotangent: float32 [32, 512, 768], P('shard', 'context'), may hold values from -6 to 6
Outputs:
- outputs: float32 [32, 512, 768], P('shard', 'context')
- input_grad: float32 [32, 512, 768], P('shard', 'context')
- grad_projection: float32 [2, 3, 768, 768], P(None, None, 'shard', 'tensor')
- head_grad: float32 [2, 2, 12, 64], P(None, None, 'tensor', 'shard')
- grad_mixing: float32 [2, 768, 768], P(None, 'tensor', 'shard')
- grad_expansion: float32 [2, 768, 3072], P(None, 'shard', 'tensor')
- hidden_grad: float32 [2, 48, 64], P(None, 'tensor', 'shard')
- grad_contraction: float32 [2, 3072, 768], P(None, 'tensor', 'shard')
- gains_grad: float32 [2, 2, 768], P(None, None, 'shard')
- grad_offsets: float32 [2, 4, 768], P(None, None, 'shard')
Inputs may be any that keep to these rules, and one draw needn't show every extreme that they name: `segment_ids`: within a row ids never fall; every document holds 1 to 256 positions and in every row some document holds exactly 256.
All inputs are finite; a program needn't handle non-finite values.
Results may differ from a plain program's by a relative error of at most 0.033.
Values may be sent and summed in bfloat16 or wider, within the bound.
No kernel may reach another device: no remote copies, remote signals or barrier semaphores. Data moves between devices by JAX's collectives and lax.ppermute only.
A program may use at most 128 MiB of HBM per device.

v0:
```python
import jax
import jax.numpy as jnp
from jax import lax
from jax.sharding import PartitionSpec as P

HEAD = 64
EPS = 1e-05
GELU_COEF = 0.7978845608028654
GELU_CUBE = 0.044715
MASKED = -1e30
HALF = jnp.bfloat16
FULL = jnp.float32


def gelu_value(preact):
    inner_arg = GELU_COEF * (preact + GELU_CUBE * preact * preact * preact)
    return 0.5 * preact * (1.0 + jnp.tanh(inner_arg))


def gelu_slope(preact):
    inner_arg = GELU_COEF * (preact + GELU_CUBE * preact * preact * preact)
    tanh_value = jnp.tanh(inner_arg)
    return 0.5 * (1.0 + tanh_value) + 0.5 * preact * (1.0 - tanh_value * tanh_value) * GELU_COEF * (
        1.0 + 3.0 * GELU_CUBE * preact * preact
    )


def norm_forward(stream):
    center = stream - jnp.mean(stream, axis=-1, keepdims=True)
    spread = lax.rsqrt(jnp.mean(center * center, axis=-1, keepdims=True) + EPS)
    return (center * spread, spread)


def norm_backward(upstream, normed, spread, gain_row):
    scaled = upstream * gain_row
    first_mean = jnp.mean(scaled, axis=-1, keepdims=True)
    second_mean = jnp.mean(scaled * normed, axis=-1, keepdims=True)
    return spread * (scaled - first_mean - normed * second_mean)


def dot(left, right, left_dim, right_dim):
    return lax.dot_general(
        left, right, (((left_dim,), (right_dim,)), ((), ())), preferred_element_type=FULL
    )


def pair_sum(part):
    size = lax.axis_size("tensor")
    other = lax.ppermute(part, "tensor", [(i, (i + 1) % size) for i in range(size)])
    return part.astype(FULL) + other.astype(FULL)


def from_before(block, steps):
    size = lax.axis_size("context")
    return lax.ppermute(block, "context", [(i, i + steps) for i in range(size - steps)])


def from_after(block, steps):
    size = lax.axis_size("context")
    return lax.ppermute(block, "context", [(i + steps, i) for i in range(size - steps)])


def context_sum(part):
    size = lax.axis_size("context")
    total = part.astype(FULL)
    for steps in range(1, size):
        moved = lax.ppermute(part, "context", [(i, (i + steps) % size) for i in range(size)])
        total = total + moved.astype(FULL)
    return total


def masked_scores(query_block, key_block, visible, head_scale):
    scores = (
        jnp.einsum("rqhe,rkhe->rhqk", query_block, key_block, preferred_element_type=FULL)
        * head_scale
    )
    return jnp.where(visible, scores, MASKED)


def per_device(
    inputs,
    segment_ids,
    projection,
    head_bias,
    mixing,
    expansion,
    hidden_bias,
    contraction,
    norm_gains,
    offsets,
    cotangent,
):
    layers = projection.shape[0]
    rows, block, width = inputs.shape
    shards = lax.axis_size("shard")
    contexts = lax.axis_size("context")
    own = projection.shape[2]
    heads = head_bias.shape[2]
    head_cols = projection.shape[3]
    hidden = expansion.shape[2]
    tokens = rows * block
    head_scale = HEAD ** (-0.5)
    back_steps = 2
    gathered = []
    for layer in range(layers):
        packed = jnp.concatenate(
            [
                projection[layer, 0],
                projection[layer, 1],
                projection[layer, 2],
                mixing[layer].T,
                expansion[layer],
                contraction[layer].T,
            ],
            axis=1,
        )
        gathered.append(lax.all_gather(packed, "shard", axis=0, tiled=True))
    small_parts = [norm_gains, offsets, head_bias, hidden_bias]
    small_sizes = [part.size for part in small_parts]
    small_total = sum(small_sizes)
    small_padded = -(-small_total // 1024) * 1024
    small = jnp.concatenate(
        [part.reshape(-1) for part in small_parts]
        + [jnp.zeros((small_padded - small_total,), HALF)]
    )
    small = jnp.broadcast_to(small.reshape(1, -1, 128), (shards, small_padded // 128, 128))
    small = lax.all_to_all(small, "shard", 0, 0).reshape(shards, small_padded)

    def widen(index):
        start = sum(small_sizes[:index])
        shape = small_parts[index].shape
        piece = small[:, start : start + small_sizes[index]].astype(FULL).reshape((shards,) + shape)
        piece = jnp.moveaxis(piece, 0, -2)
        return piece.reshape(shape[:-1] + (shards * shape[-1],))

    gains_all, offsets_all = (widen(0), widen(1))
    head_all = widen(2).reshape(layers, 2, head_cols)
    hidden_all = widen(3).reshape(layers, hidden)
    seg_before = [from_before(segment_ids, steps) for steps in range(back_steps, 0, -1)]
    segments_all = jnp.concatenate(seg_before + [segment_ids], axis=1)
    query_pos = jnp.arange(block, dtype=jnp.int32) + back_steps * block
    key_pos = jnp.arange((back_steps + 1) * block, dtype=jnp.int32)
    first_key = (back_steps - lax.axis_index("context")) * block
    visible = (
        (segments_all[:, None, :] == segment_ids[:, :, None])
        & (key_pos[None, None, :] <= query_pos[None, :, None])
        & (key_pos >= first_key)[None, None, :]
    )
    visible = visible[:, None]

    def split_weights(weights):
        ends = [3 * head_cols, 4 * head_cols, 4 * head_cols + hidden, 4 * head_cols + 2 * hidden]
        return (
            weights[:, : ends[0]],
            weights[:, ends[0] : ends[1]],
            weights[:, ends[1] : ends[2]],
            weights[:, ends[2] : ends[3]],
        )

    stream = inputs.reshape(tokens, width)
    kept = []
    for layer in range(layers):
        qkv_weight, out_weight, up_weight, down_weight = split_weights(gathered[layer])
        gain, offset = (gains_all[layer], offsets_all[layer])
        normed_one, spread_one = norm_forward(stream)
        attend_input = (normed_one * gain[0] + offset[0]).astype(HALF)
        zero_bias = jnp.zeros((head_cols,), FULL)
        bias = jnp.concatenate([head_all[layer, 0], zero_bias, head_all[layer, 1]])
        projected = (dot(attend_input, qkv_weight, 1, 0) + bias).astype(HALF)
        query_rows = projected[:, :head_cols]
        key_value = projected[:, head_cols:].reshape(rows, block, 2 * head_cols)
        before = [from_before(key_value, steps) for steps in range(back_steps, 0, -1)]
        key_value_all = jnp.concatenate(before + [key_value], axis=1)
        query_block = query_rows.reshape(rows, block, heads, HEAD)
        key_block = key_value_all[:, :, :head_cols].reshape(rows, -1, heads, HEAD)
        value_block = key_value_all[:, :, head_cols:].reshape(rows, -1, heads, HEAD)
        masked = masked_scores(query_block, key_block, visible, head_scale)
        row_top = jnp.max(masked, axis=-1, keepdims=True)
        log_total = row_top + jnp.log(jnp.sum(jnp.exp(masked - row_top), axis=-1, keepdims=True))
        soft_half = jnp.exp(masked - log_total).astype(HALF)
        attended = (
            jnp.einsum("rhqk,rkhe->rqhe", soft_half, value_block, preferred_element_type=FULL)
            .astype(HALF)
            .reshape(tokens, head_cols)
        )
        middle = stream + pair_sum(dot(attended, out_weight, 1, 1)) + offset[2]
        normed_two, spread_two = norm_forward(middle)
        feed_input = (normed_two * gain[1] + offset[1]).astype(HALF)
        preact = dot(feed_input, up_weight, 1, 0) + hidden_all[layer]
        activation = gelu_value(preact).astype(HALF)
        stream = middle + pair_sum(dot(activation, down_weight, 1, 1)) + offset[3]
        kept.append(
            (
                normed_one,
                spread_one,
                attend_input,
                query_block,
                key_block,
                value_block,
                log_total,
                attended,
                normed_two,
                spread_two,
                feed_input,
                preact,
                activation,
            )
        )

    def scatter(parts):
        packed = jnp.concatenate([part.astype(HALF) for part in parts], axis=1)
        return lax.psum_scatter(packed, "shard", scatter_dimension=0, tiled=True)

    upstream = cotangent.reshape(tokens, width)
    feed_shares, attend_shares, vectors = ([None] * layers, [None] * layers, [None] * layers)
    for layer in reversed(range(layers)):
        (
            normed_one,
            spread_one,
            attend_input,
            query_block,
            key_block,
            value_block,
            log_total,
            attended,
            normed_two,
            spread_two,
            feed_input,
            preact,
            activation,
        ) = kept[layer]
        qkv_weight, out_weight, up_weight, down_weight = split_weights(gathered[layer])
        gain = gains_all[layer]
        upstream_half = upstream.astype(HALF)
        contraction_part = dot(upstream_half, activation, 0, 0)
        offset_down = jnp.sum(upstream, axis=0)
        hidden_back = dot(upstream_half, down_weight, 1, 0) * gelu_slope(preact)
        hidden_half = hidden_back.astype(HALF)
        hidden_part = jnp.sum(hidden_back, axis=0)
        expansion_part = dot(feed_input, hidden_half, 0, 0)
        feed_shares[layer] = scatter([expansion_part, contraction_part])
        feed_back = pair_sum(dot(hidden_half, up_weight, 1, 1).astype(HALF))
        gain_two = jnp.sum(feed_back * normed_two, axis=0)
        offset_two = jnp.sum(feed_back, axis=0)
        middle_back = upstream + norm_backward(feed_back, normed_two, spread_two, gain[1])
        middle_half = middle_back.astype(HALF)
        mixing_part = dot(middle_half, attended, 0, 0)
        offset_mix = jnp.sum(middle_back, axis=0)
        attended_back = dot(middle_half, out_weight, 1, 0).astype(HALF)
        back_heads = attended_back.reshape(rows, block, heads, HEAD)
        attended_heads = attended.reshape(rows, block, heads, HEAD)
        row_delta = jnp.sum(back_heads.astype(FULL) * attended_heads.astype(FULL), axis=-1)
        masked = masked_scores(query_block, key_block, visible, head_scale)
        soft = jnp.exp(masked - log_total)
        soft_half = soft.astype(HALF)
        prob_back = jnp.einsum(
            "rqhe,rkhe->rhqk", back_heads, value_block, preferred_element_type=FULL
        )
        score_back = (
            soft * (prob_back - jnp.transpose(row_delta, (0, 2, 1))[..., None]) * head_scale
        ).astype(HALF)
        query_back = jnp.einsum(
            "rhqk,rkhe->rqhe", score_back, key_block, preferred_element_type=FULL
        ).reshape(tokens, head_cols)
        key_full = jnp.einsum(
            "rhqk,rqhe->rkhe", score_back, query_block, preferred_element_type=FULL
        ).reshape(rows, -1, head_cols)
        value_full = jnp.einsum(
            "rhqk,rqhe->rkhe", soft_half, back_heads, preferred_element_type=FULL
        ).reshape(rows, -1, head_cols)
        both_full = jnp.concatenate([key_full, value_full], axis=2)
        both_back = both_full[:, back_steps * block :]
        for steps in range(1, back_steps + 1):
            start = (back_steps - steps) * block
            both_back = both_back + from_after(
                both_full[:, start : start + block].astype(HALF), steps
            ).astype(FULL)
        both_back = both_back.reshape(tokens, 2 * head_cols)
        head_part = jnp.concatenate(
            [jnp.sum(query_back, axis=0), jnp.sum(both_back[:, head_cols:], axis=0)]
        )
        project_back = jnp.concatenate([query_back, both_back], axis=1).astype(HALF)
        projection_part = dot(attend_input, project_back, 0, 0)
        attend_shares[layer] = scatter([projection_part, mixing_part])
        input_back = pair_sum(dot(project_back, qkv_weight, 1, 1).astype(HALF))
        gain_one = jnp.sum(input_back * normed_one, axis=0)
        offset_one = jnp.sum(input_back, axis=0)
        upstream = middle_back + norm_backward(input_back, normed_one, spread_one, gain[0])
        vectors[layer] = (
            [gain_one, gain_two],
            [offset_one, offset_two, offset_mix, offset_down],
            head_part,
            hidden_part,
        )

    def spread_out(values, shape):
        lead = shape[:-1]
        values = values.reshape(lead + (shards, shape[-1]))
        return jnp.moveaxis(values, -2, 0).reshape(shards, -1)

    gain_sums = jnp.stack([jnp.stack(entry[0]) for entry in vectors])
    offset_sums = jnp.stack([jnp.stack(entry[1]) for entry in vectors])
    head_sums = jnp.stack([entry[2] for entry in vectors])
    hidden_sums = jnp.stack([entry[3] for entry in vectors])
    vector_pack = jnp.concatenate(
        [
            spread_out(values, part.shape)
            for values, part in zip((gain_sums, offset_sums, head_sums, hidden_sums), small_parts)
        ]
        + [jnp.zeros((shards, small_padded - small_total), FULL)],
        axis=1,
    )
    vector_pack = lax.all_to_all(vector_pack.reshape(shards, -1, 128), "shard", 0, 0)
    vector_own = context_sum(jnp.sum(vector_pack, axis=0)).reshape(-1)
    vector_out = []
    for index, part in enumerate(small_parts):
        start = sum(small_sizes[:index])
        vector_out.append(vector_own[start : start + small_sizes[index]].reshape(part.shape))
    gains_grad, offsets_grad, head_grad, hidden_grad = vector_out
    feed_own = [context_sum(share) for share in feed_shares]
    attend_own = [context_sum(share) for share in attend_shares]
    projection_grad = jnp.stack(
        [
            jnp.stack([share[:, k * head_cols : (k + 1) * head_cols] for k in range(3)])
            for share in attend_own
        ]
    )
    mixing_grad = jnp.stack([share[:, 3 * head_cols :].T for share in attend_own])
    expansion_grad = jnp.stack([share[:, :hidden] for share in feed_own])
    contraction_grad = jnp.stack([share[:, hidden:].T for share in feed_own])
    return (
        stream.reshape(rows, block, width),
        upstream.reshape(rows, block, width),
        projection_grad,
        head_grad,
        mixing_grad,
        expansion_grad,
        hidden_grad,
        contraction_grad,
        gains_grad,
        offsets_grad,
    )


def solution(mesh):
    in_specs = (
        P("shard", "context", None),
        P("shard", "context"),
        P(None, None, "shard", "tensor"),
        P(None, None, "tensor", "shard"),
        P(None, "tensor", "shard"),
        P(None, "shard", "tensor"),
        P(None, "tensor", "shard"),
        P(None, "tensor", "shard"),
        P(None, None, "shard"),
        P(None, None, "shard"),
        P("shard", "context", None),
    )
    out_specs = (
        P("shard", "context", None),
        P("shard", "context", None),
        P(None, None, "shard", "tensor"),
        P(None, None, "tensor", "shard"),
        P(None, "tensor", "shard"),
        P(None, "shard", "tensor"),
        P(None, "tensor", "shard"),
        P(None, "tensor", "shard"),
        P(None, None, "shard"),
        P(None, None, "shard"),
    )
    return jax.shard_map(
        per_device, mesh=mesh, in_specs=in_specs, out_specs=out_specs, check_vma=False
    )
```

profile of v0, /device:TPU:0, one launch (start us, length us, event | category | flops | bytes accessed | tf_op | source)
XLA Modules:
  0.0 616.7 jit_solution(8124101954752828164)
XLA Ops:
  14.1 5.2 collective-permute-start.2
  23.3 7.9 %all-to-all-start = ((bf16[16,8,128]{2,1,0:T(8,128)(2,1)}), bf16[16,8,128]{2,1,0:T(8,128)(2,1)S(1)}, u32[]{:S(2)}, u32[]{:S(2)}) async-start(bf16[16,8,128]{2,1,0:T(8,128)(2,1)} %broadcast_in_dim.34), calls=%async_computation | async-start | bytes 65536 | tf_op jit(solution)/shard_map/all_to_all | solution.py:127
  31.7 7.1 %all-to-all-done = bf16[16,8,128]{2,1,0:T(8,128)(2,1)S(1)} async-done(((bf16[16,8,128]{2,1,0:T(8,128)(2,1)}), bf16[16,8,128]{2,1,0:T(8,128)(2,1)S(1)}, u32[]{:S(2)}, u32[]{:S(2)}) %all-to-all-start) | async-done | bytes 32800 | tf_op jit(solution)/shard_map/all_to_all | solution.py:127
  42.3 39.0 %all-gather.3.cloned.1.call-done = bf16[768,4608]{1,0:T(8,128)(2,1)} async-done(((bf16[48,4608]{1,0:T(8,128)(2,1)}), bf16[768,4608]{1,0:T(8,128)(2,1)}) %all-gather.3.cloned.1.call-update) | async-done | bytes 7077904 | tf_op jit(solution)/shard_map/all_gather | solution.py:117
  83.5 4.9 collective-permute-start
  91.4 6.5 %collective-permute-done = bf16[2,128,768]{2,1,0:T(8,128)(2,1)S(1)} collective-permute-done((bf16[2,128,768]{2,1,0:T(8,128)(2,1)S(1)}, bf16[2,128,768]{2,1,0:T(8,128)(2,1)S(1)}, u32[]{:S(2)}, u32[]{:S(2)}) %collective-permute-start) | collective-permute-done | bytes 393248 | tf_op jit(solution)/shard_map/ppermute | solution.py:55
  97.9 7.3 %collective-permute-done.1 = bf16[2,128,768]{2,1,0:T(8,128)(2,1)S(1)} collective-permute-done((bf16[2,128,768]{2,1,0:T(8,128)(2,1)S(1)}, bf16[2,128,768]{2,1,0:T(8,128)(2,1)S(1)}, u32[]{:S(2)}, u32[]{:S(2)}) %collective-permute-start.1) | collective-permute-done | bytes 393248 | tf_op jit(solution)/shard_map/ppermute | solution.py:55
  128.6 4.2 fusion.15
  138.5 10.1 %all-gather.5.cloned.1.call-done = bf16[768,4608]{1,0:T(8,128)(2,1)} async-done(((bf16[48,4608]{1,0:T(8,128)(2,1)}), bf16[768,4608]{1,0:T(8,128)(2,1)}) %all-gather.5.cloned.1.call-update) | async-done | bytes 7077904 | tf_op jit(solution)/shard_map/all_gather | solution.py:117
  151.9 5.7 collective-permute-start.6
  162.8 3.9 collective-permute-done.6
  166.7 7.3 %collective-permute-done.7 = bf16[2,128,768]{2,1,0:T(8,128)(2,1)} collective-permute-done((bf16[2,128,768]{2,1,0:T(8,128)(2,1)}, bf16[2,128,768]{2,1,0:T(8,128)(2,1)}, u32[]{:S(2)}, u32[]{:S(2)}) %collective-permute-start.7) | collective-permute-done | bytes 393248 | tf_op jit(solution)/shard_map/ppermute | solution.py:55
  203.6 4.2 fusion.135
  246.2 7.9 %collective-permute-done.11 = bf16[2,128,768]{2,1,0:T(8,128)(2,1)} collective-permute-done((bf16[2,128,768]{2,1,0:T(8,128)(2,1)}, bf16[2,128,768]{2,1,0:T(8,128)(2,1)}, u32[]{:S(2)}, u32[]{:S(2)}) %collective-permute-start.11) | collective-permute-done | bytes 393248 | tf_op jit(solution)/shard_map/ppermute | solution.py:60
  298.5 15.0 %collective-permute-done.15 = bf16[2,128,768]{2,1,0:T(8,128)(2,1)} collective-permute-done((bf16[2,128,768]{2,1,0:T(8,128)(2,1)}, bf16[2,128,768]{2,1,0:T(8,128)(2,1)}, u32[]{:S(2)}, u32[]{:S(2)}) %collective-permute-start.15) | collective-permute-done | bytes 393248 | tf_op jit(solution)/shard_map/ppermute | solution.py:60
  352.5 5.3 all-to-all-start.1
  357.8 7.6 %all-to-all-done.1 = f32[16,8,128]{2,1,0:T(8,128)S(1)} async-done(((f32[16,8,128]{2,1,0:T(8,128)}), f32[16,8,128]{2,1,0:T(8,128)S(1)}, u32[]{:S(2)}, u32[]{:S(2)}) %all-to-all-start.1) | async-done | bytes 65568 | tf_op jit(solution)/shard_map/all_to_all | solution.py:313
  365.5 7.0 %collective-permute-start.24 = (f32[8,128]{1,0:T(8,128)S(1)}, f32[8,128]{1,0:T(8,128)S(1)}, u32[]{:S(2)}, u32[]{:S(2)}) collective-permute-start(f32[8,128]{1,0:T(8,128)S(1)} %reduce_sum.395), channel_id=1, source_target_pairs={{0,2},{2,4},{4,6},{6,0},{1,3},{3,5},{5,7},{7,1},{8,10},{10,12},{12... | collective-permute-start | bytes 12296 | tf_op jit(solution)/shard_map/ppermute | solution.py:67
  388.0 41.1 %reduce-scatter.5.cloned.1.call-done = bf16[48,1536]{1,0:T(8,128)(2,1)} async-done(((bf16[768,1536]{1,0:T(8,128)(2,1)}), bf16[48,1536]{1,0:T(8,128)(2,1)}) %reduce-scatter.5.cloned.1.call-update) | async-done | bytes 147472 | tf_op jit(solution)/shard_map/reduce_scatter | solution.py:212
  439.6 70.3 %reduce-scatter.11.cloned.1.call-done = bf16[48,3072]{1,0:T(8,128)(2,1)} async-done(((bf16[768,3072]{1,0:T(8,128)(2,1)}), bf16[48,3072]{1,0:T(8,128)(2,1)}) %reduce-scatter.11.cloned.1.call-update) | async-done | bytes 294928 | tf_op jit(solution)/shard_map/reduce_scatter | solution.py:212
  520.3 5.5 collective-permute-done.31
  526.0 64.9 %reduce-scatter.9.cloned.1.call-done = bf16[48,3072]{1,0:T(8,128)(2,1)} async-done(((bf16[768,3072]{1,0:T(8,128)(2,1)}), bf16[48,3072]{1,0:T(8,128)(2,1)}) %reduce-scatter.9.cloned.1.call-update) | async-done | bytes 294928 | tf_op jit(solution)/shard_map/reduce_scatter | solution.py:212
  596.5 4.8 collective-permute-done.27
  601.3 5.5 collective-permute-done.28
  (538 shorter events, 252.4 us)
Async XLA Ops:
  7.2 74.0 %all-gather.3.cloned.1.call-start = ((), (), s32[]{:S(2)}) async-start(), calls=%async_computation.6 | async-start | bytes 7520256 | tf_op jit(solution)/shard_map/all_gather | solution.py:117
  13.4 135.2 %all-gather.5.cloned.1.call-start = ((), (), s32[]{:S(2)}) async-start(), calls=%async_computation.7 | async-start | bytes 7520256 | tf_op jit(solution)/shard_map/all_gather | solution.py:117
  14.1 76.8 %collective-permute-start.2 = (s32[2,128]{1,0:T(2,128)S(1)}, s32[2,128]{1,0:T(2,128)S(1)}, u32[]{:S(2)}, u32[]{:S(2)}) collective-permute-start(s32[2,128]{1,0:T(2,128)S(1)} %copy-done.105), channel_id=1, source_target_pairs={{0,4},{2,6},{1,5},{3,7},{8,12},{10,14},{9,13},{11,15},{16,20},{18,... | collective-permute-start | bytes 3080 | tf_op jit(solution)/shard_map/ppermute | solution.py:55
  19.3 71.7 %collective-permute-start.3 = (s32[2,128]{1,0:T(2,128)S(1)}, s32[2,128]{1,0:T(2,128)S(1)}, u32[]{:S(2)}, u32[]{:S(2)}) collective-permute-start(s32[2,128]{1,0:T(2,128)S(1)} %copy-done.105), channel_id=1, source_target_pairs={{0,2},{2,4},{4,6},{1,3},{3,5},{5,7},{8,10},{10,12},{12,14},{9,11},... | collective-permute-start | bytes 3080 | tf_op jit(solution)/shard_map/ppermute | solution.py:55
  23.3 15.6 %all-to-all-start = ((bf16[16,8,128]{2,1,0:T(8,128)(2,1)}), bf16[16,8,128]{2,1,0:T(8,128)(2,1)S(1)}, u32[]{:S(2)}, u32[]{:S(2)}) async-start(bf16[16,8,128]{2,1,0:T(8,128)(2,1)} %broadcast_in_dim.34), calls=%async_computation | async-start | bytes 65536 | tf_op jit(solution)/shard_map/all_to_all | solution.py:127
  31.2 346.6 %reduce-scatter.7.cloned.1.call-start = ((), (), s32[]{:S(2)}) async-start(), calls=%async_computation.9 | async-start | bytes 2506752 | tf_op jit(solution)/shard_map/reduce_scatter | solution.py:212
  83.5 14.5 %collective-permute-start = (bf16[2,128,768]{2,1,0:T(8,128)(2,1)S(1)}, bf16[2,128,768]{2,1,0:T(8,128)(2,1)S(1)}, u32[]{:S(2)}, u32[]{:S(2)}) collective-permute-start(bf16[2,128,768]{2,1,0:T(8,128)(2,1)S(1)} %bitcast.247), channel_id=1, source_target_pairs={{0,4},{2,6},{1,5},{3,7},{8,12},{10,14},{9,13},{11,15},{16,20},{18,... | collective-permute-start | bytes 1179656 | tf_op jit(solution)/shard_map/ppermute | solution.py:55
  88.4 16.8 %collective-permute-start.1 = (bf16[2,128,768]{2,1,0:T(8,128)(2,1)S(1)}, bf16[2,128,768]{2,1,0:T(8,128)(2,1)S(1)}, u32[]{:S(2)}, u32[]{:S(2)}) collective-permute-start(bf16[2,128,768]{2,1,0:T(8,128)(2,1)S(1)} %bitcast.248), channel_id=1, source_target_pairs={{0,2},{2,4},{4,6},{1,3},{3,5},{5,7},{8,10},{10,12},{12,14},{9,11},... | collective-permute-start | bytes 1179656 | tf_op jit(solution)/shard_map/ppermute | solution.py:55
  151.9 14.8 %collective-permute-start.6 = (bf16[2,128,768]{2,1,0:T(8,128)(2,1)}, bf16[2,128,768]{2,1,0:T(8,128)(2,1)}, u32[]{:S(2)}, u32[]{:S(2)}) collective-permute-start(bf16[2,128,768]{2,1,0:T(8,128)(2,1)} %bitcast.30), channel_id=1, source_target_pairs={{0,4},{2,6},{1,5},{3,7},{8,12},{10,14},{9,13},{11,15},{16,20},{18,... | collective-permute-start | bytes 1179656 | tf_op jit(solution)/shard_map/ppermute | solution.py:55
  157.6 16.4 %collective-permute-start.7 = (bf16[2,128,768]{2,1,0:T(8,128)(2,1)}, bf16[2,128,768]{2,1,0:T(8,128)(2,1)}, u32[]{:S(2)}, u32[]{:S(2)}) collective-permute-start(bf16[2,128,768]{2,1,0:T(8,128)(2,1)} %bitcast.30), channel_id=1, source_target_pairs={{0,2},{2,4},{4,6},{1,3},{3,5},{5,7},{8,10},{10,12},{12,14},{9,11},... | collective-permute-start | bytes 1179656 | tf_op jit(solution)/shard_map/ppermute | solution.py:55
  239.6 14.4 %collective-permute-start.11 = (bf16[2,128,768]{2,1,0:T(8,128)(2,1)}, bf16[2,128,768]{2,1,0:T(8,128)(2,1)}, u32[]{:S(2)}, u32[]{:S(2)}) collective-permute-start(bf16[2,128,768]{2,1,0:T(8,128)(2,1)} %get-tuple-element.106), channel_id=1, source_target_pairs={{2,0},{4,2},{6,4},{3,1},{5,3},{7,5},{10,8},{12,10},{14,12},{11,9},... | collective-permute-start | bytes 1179656 | tf_op jit(solution)/shard_map/ppermute | solution.py:60
  240.9 16.2 %collective-permute-start.12 = (bf16[2,128,768]{2,1,0:T(8,128)(2,1)}, bf16[2,128,768]{2,1,0:T(8,128)(2,1)}, u32[]{:S(2)}, u32[]{:S(2)}) collective-permute-start(bf16[2,128,768]{2,1,0:T(8,128)(2,1)} %get-tuple-element.107), channel_id=1, source_target_pairs={{4,0},{6,2},{5,1},{7,3},{12,8},{14,10},{13,9},{15,11},{20,16},{22,... | collective-permute-start | bytes 1179656 | tf_op jit(solution)/shard_map/ppermute | solution.py:60
  271.7 157.4 %reduce-scatter.5.cloned.1.call-start = ((), (), s32[]{:S(2)}) async-start(), calls=%async_computation.8 | async-start | bytes 2506752 | tf_op jit(solution)/shard_map/reduce_scatter | solution.py:212
  293.6 20.0 %collective-permute-start.15 = (bf16[2,128,768]{2,1,0:T(8,128)(2,1)}, bf16[2,128,768]{2,1,0:T(8,128)(2,1)}, u32[]{:S(2)}, u32[]{:S(2)}) collective-permute-start(bf16[2,128,768]{2,1,0:T(8,128)(2,1)} %get-tuple-element.104), channel_id=1, source_target_pairs={{2,0},{4,2},{6,4},{3,1},{5,3},{7,5},{10,8},{12,10},{14,12},{11,9},... | collective-permute-start | bytes 1179656 | tf_op jit(solution)/shard_map/ppermute | solution.py:60
  294.9 21.9 %collective-permute-start.16 = (bf16[2,128,768]{2,1,0:T(8,128)(2,1)}, bf16[2,128,768]{2,1,0:T(8,128)(2,1)}, u32[]{:S(2)}, u32[]{:S(2)}) collective-permute-start(bf16[2,128,768]{2,1,0:T(8,128)(2,1)} %get-tuple-element.105), channel_id=1, source_target_pairs={{4,0},{6,2},{5,1},{7,3},{12,8},{14,10},{13,9},{15,11},{20,16},{22,... | collective-permute-start | bytes 1179656 | tf_op jit(solution)/shard_map/ppermute | solution.py:60
  321.3 188.7 %reduce-scatter.11.cloned.1.call-start = ((), (), s32[]{:S(2)}) async-start(), calls=%async_computation.11 | async-start | bytes 5013504 | tf_op jit(solution)/shard_map/reduce_scatter | solution.py:212
  328.2 262.7 %reduce-scatter.9.cloned.1.call-start = ((), (), s32[]{:S(2)}) async-start(), calls=%async_computation.10 | async-start | bytes 5013504 | tf_op jit(solution)/shard_map/reduce_scatter | solution.py:212
  352.5 12.9 %all-to-all-start.1 = ((f32[16,8,128]{2,1,0:T(8,128)}), f32[16,8,128]{2,1,0:T(8,128)S(1)}, u32[]{:S(2)}, u32[]{:S(2)}) async-start(f32[16,8,128]{2,1,0:T(8,128)} %bitcast.123), calls=%async_computation.3 | async-start | bytes 131072 | tf_op jit(solution)/shard_map/all_to_all | solution.py:313
  365.5 11.0 %collective-permute-start.24 = (f32[8,128]{1,0:T(8,128)S(1)}, f32[8,128]{1,0:T(8,128)S(1)}, u32[]{:S(2)}, u32[]{:S(2)}) collective-permute-start(f32[8,128]{1,0:T(8,128)S(1)} %reduce_sum.395), channel_id=1, source_target_pairs={{0,2},{2,4},{4,6},{6,0},{1,3},{3,5},{5,7},{7,1},{8,10},{10,12},{12... | collective-permute-start | bytes 12296 | tf_op jit(solution)/shard_map/ppermute | solution.py:67
  511.4 14.4 %collective-permute-start.31 = (bf16[48,3072]{1,0:T(8,128)(2,1)}, bf16[48,3072]{1,0:T(8,128)(2,1)S(1)}, u32[]{:S(2)}, u32[]{:S(2)}) collective-permute-start(bf16[48,3072]{1,0:T(8,128)(2,1)} %reduce-scatter.11.cloned.1.call-done), channel_id=1, source_target_pairs={{0,4},{2,6},{4,0},{6,2},{1,5},{3,7},{5,1},{7,3},{8,12},{10,14},{12... | collective-permute-start | bytes 884744 | tf_op jit(solution)/shard_map/ppermute | solution.py:67
  514.1 11.7 %collective-permute-start.32 = (bf16[48,3072]{1,0:T(8,128)(2,1)}, bf16[48,3072]{1,0:T(8,128)(2,1)S(1)}, u32[]{:S(2)}, u32[]{:S(2)}) collective-permute-start(bf16[48,3072]{1,0:T(8,128)(2,1)} %reduce-scatter.11.cloned.1.call-done), channel_id=1, source_target_pairs={{0,6},{2,0},{4,2},{6,4},{1,7},{3,1},{5,3},{7,5},{8,14},{10,8},{12,... | collective-permute-start | bytes 884744 | tf_op jit(solution)/shard_map/ppermute | solution.py:67
  590.9 10.4 %collective-permute-start.27 = (bf16[48,3072]{1,0:T(8,128)(2,1)}, bf16[48,3072]{1,0:T(8,128)(2,1)S(1)}, u32[]{:S(2)}, u32[]{:S(2)}) collective-permute-start(bf16[48,3072]{1,0:T(8,128)(2,1)} %reduce-scatter.9.cloned.1.call-done), channel_id=1, source_target_pairs={{0,2},{2,4},{4,6},{6,0},{1,3},{3,5},{5,7},{7,1},{8,10},{10,12},{12... | collective-permute-start | bytes 884744 | tf_op jit(solution)/shard_map/ppermute | solution.py:67
  592.3 14.4 %collective-permute-start.28 = (bf16[48,3072]{1,0:T(8,128)(2,1)}, bf16[48,3072]{1,0:T(8,128)(2,1)S(1)}, u32[]{:S(2)}, u32[]{:S(2)}) collective-permute-start(bf16[48,3072]{1,0:T(8,128)(2,1)} %reduce-scatter.9.cloned.1.call-done), channel_id=1, source_target_pairs={{0,4},{2,6},{4,0},{6,2},{1,5},{3,7},{5,1},{7,3},{8,12},{10,14},{12... | collective-permute-start | bytes 884744 | tf_op jit(solution)/shard_map/ppermute | solution.py:67
  595.0 11.7 %collective-permute-start.29 = (bf16[48,3072]{1,0:T(8,128)(2,1)}, bf16[48,3072]{1,0:T(8,128)(2,1)S(1)}, u32[]{:S(2)}, u32[]{:S(2)}) collective-permute-start(bf16[48,3072]{1,0:T(8,128)(2,1)} %reduce-scatter.9.cloned.1.call-done), channel_id=1, source_target_pairs={{0,6},{2,0},{4,2},{6,4},{1,7},{3,1},{5,3},{7,5},{8,14},{10,8},{12,... | collective-permute-start | bytes 884744 | tf_op jit(solution)/shard_map/ppermute | solution.py:67
  (136 other events, 931.3 us)
Sparse Core Ops, SparseCore 0:
  13.5 67.7 all-gather.2
  83.9 64.6 all-gather.4
  271.8 79.7 reduce-scatter.6
  354.8 74.2 reduce-scatter.4
  432.3 77.6 reduce-scatter.10
  513.1 77.6 reduce-scatter.8
where the time goes:
time: 627 us; the launch traced here: 617 us
  waiting for transfers between devices  323 us (52%)
  local copies, waits for them, and re-layouts  82.9 us (13%)
  starting transfers between devices  76.2 us (12%)
  matrix products  68.4 us (11%)
  other arithmetic  50.4 us (8%)
  between operations  16.2 us (3%)
    reduce_scatter x4, waiting for transfers between devices, scatter(): return lax.psum_scatter(packed, 'shard', scatter_dimension=0, tiled=True)  176 us
    all_gather x2, waiting for transfers between devices, per_device(): gathered.append(lax.all_gather(packed, 'shard', axis=0, tiled=True))  49.1 us
    dot_general x24, matrix products, dot(): lax.dot_general(left, right, (((left_dim,), (right_dim,)), ((), ())), pre...  46.1 us
    ppermute x15, starting transfers between devices, context_sum(): lax.ppermute(part, 'context', [(i, (i + steps) % size) for i in range(siz...  31.3 us
    ppermute x4, waiting for transfers between devices, from_after(): lax.ppermute(block, 'context', [(i + steps, i) for i in range(size - step...  29.2 us
    ppermute x15, waiting for transfers between devices, context_sum(): lax.ppermute(part, 'context', [(i, (i + steps) % size) for i in range(siz...  25.6 us
    ppermute x6, waiting for transfers between devices, from_before(): lax.ppermute(block, 'context', [(i, i + steps) for i in range(size - step...  25 us
    ppermute x6, starting transfers between devices, from_before(): lax.ppermute(block, 'context', [(i, i + steps) for i in range(size - step...  24.3 us
  transfers between devices with their start and end apart: 41, of which 26 were waited for; matrix products, arithmetic and copies ran while one was open for 19% of the time, Pallas kernels for 0%

commit v1 on v0

--- a/solution.py
+++ b/solution.py
@@ -114,7 +114,13 @@
             ],
             axis=1,
         )
-        gathered.append(lax.all_gather(packed, "shard", axis=0, tiled=True))
+
+        def put_entries_in(tile_in):
+            shard_axis = "shard"
+            t_next = jnp.concatenate(jax.lax.axis_size(shard_axis) * [tile_in], 0)
+            return jax.lax.all_to_all(t_next, shard_axis, split_axis=0, concat_axis=0, tiled=True)
+
+        gathered.append(put_entries_in(packed))
     small_parts = [norm_gains, offsets, head_bias, hidden_bias]
     small_sizes = [part.size for part in small_parts]
     small_total = sum(small_sizes)

time: 627 us -> 819 us (1.31)
  local copies, waits for them, and re-layouts: 82.9 us -> 173 us
  waiting for transfers between devices: 323 us -> 383 us
  matrix products: 68.4 us -> 85.4 us
  starting transfers between devices: 76.2 us -> 91.1 us
  other arithmetic: 50.4 us -> 58.9 us
    all_to_all x0 -> x2, waiting for transfers between devices: none -> 143 us  [put_entries_in(): jax.lax.all_to_all(t_next, shard_axis, split_axis=0, concat_axis=0, tiled...]
    unnamed x253 -> x292, local copies, waits for them, and re-layouts: 22.8 us -> 108 us
    all_gather x2 -> x0, waiting for transfers between devices: 49.1 us -> none  [per_device(): gathered.append(lax.all_gather(packed, 'shard', axis=0, tiled=True))]
    reduce_scatter x4, waiting for transfers between devices: 176 us -> 162 us  [scatter(): return lax.psum_scatter(packed, 'shard', scatter_dimension=0, tiled=True)]
    all_to_all x0 -> x2, starting transfers between devices: none -> 12.8 us  [put_entries_in(): jax.lax.all_to_all(t_next, shard_axis, split_axis=0, concat_axis=0, tiled...]
    dot_general x24, matrix products: 46.1 us -> 57.6 us  [dot(): lax.dot_general(left, right, (((left_dim,), (right_dim,)), ((), ())), pre...]
  transfers between devices with their start and end apart: 41 -> 41, of which waited for: 26 -> 26; matrix products, arithmetic and copies ran while one was open for 19% -> 28% of each run, Pallas kernels for 0% -> 0%
where the time goes in v1:
time: 819 us; the launch traced here: 807 us
  waiting for transfers between devices  383 us (47%)
  local copies, waits for them, and re-layouts  173 us (21%)
  starting transfers between devices  91.1 us (11%)
  matrix products  85.4 us (10%)
  other arithmetic  58.9 us (7%)
  between operations  15.4 us (2%)
    reduce_scatter x4, waiting for transfers between devices, scatter(): return lax.psum_scatter(packed, 'shard', scatter_dimension=0, tiled=True)  162 us
    all_to_all x2, waiting for transfers between devices, put_entries_in(): jax.lax.all_to_all(t_next, shard_axis, split_axis=0, concat_axis=0, tiled...  143 us
    unnamed x292, local copies, waits for them, and re-layouts  108 us
    dot_general x24, matrix products, dot(): lax.dot_general(left, right, (((left_dim,), (right_dim,)), ((), ())), pre...  57.6 us
    ppermute x15, starting transfers between devices, context_sum(): lax.ppermute(part, 'context', [(i, (i + steps) % size) for i in range(siz...  31.9 us
    ppermute x6, starting transfers between devices, from_before(): lax.ppermute(block, 'context', [(i, i + steps) for i in range(size - step...  25.4 us
    ppermute x4, waiting for transfers between devices, from_after(): lax.ppermute(block, 'context', [(i + steps, i) for i in range(size - step...  25 us
    ppermute x15, waiting for transfers between devices, context_sum(): lax.ppermute(part, 'context', [(i, (i + steps) % size) for i in range(siz...  24.8 us
  transfers between devices with their start and end apart: 41, of which 26 were waited for; matrix products, arithmetic and copies ran while one was open for 28% of the time, Pallas kernels for 0%

profile of v1, /device:TPU:0, one launch (start us, length us, event | category | flops | bytes accessed | tf_op | source)
XLA Modules:
  0.0 806.6 jit_solution(5356846772452119528)
XLA Ops:
  11.4 8.0 all-to-all-start
  112.3 7.4 all-to-all-start.1
  119.7 5.1 collective-permute-start.2
  130.1 93.4 %all-to-all-done.1 = bf16[16,48,4608]{2,1,0:T(8,128)(2,1)} async-done(((bf16[16,48,4608]{2,1,0:T(8,128)(2,1)}), bf16[16,48,4608]{2,1,0:T(8,128)(2,1)}, u32[]{:S(2)}, u32[]{:S(2)}) %all-to-all-start.1) | async-done | bytes 7077920 | tf_op jit(solution)/shard_map/all_to_all | solution.py:121
  223.5 5.4 all-to-all-start.2
  231.7 5.1 collective-permute-start
  240.6 5.8 collective-permute-done
  247.1 4.5 collective-permute-done.1
  271.2 4.2 fusion.15
  281.1 49.2 %all-to-all-done.2 = bf16[16,48,4608]{2,1,0:T(8,128)(2,1)} async-done(((bf16[16,48,4608]{2,1,0:T(8,128)(2,1)}), bf16[16,48,4608]{2,1,0:T(8,128)(2,1)}, u32[]{:S(2)}, u32[]{:S(2)}) %all-to-all-start.2) | async-done | bytes 7077920 | tf_op jit(solution)/shard_map/all_to_all | solution.py:121
  333.6 5.9 collective-permute-start.6
  348.5 4.4 collective-permute-done.7
  383.1 4.2 fusion.135
  433.5 6.3 collective-permute-done.11
  493.4 12.8 %collective-permute-done.15 = bf16[2,128,768]{2,1,0:T(8,128)(2,1)} collective-permute-done((bf16[2,128,768]{2,1,0:T(8,128)(2,1)}, bf16[2,128,768]{2,1,0:T(8,128)(2,1)}, u32[]{:S(2)}, u32[]{:S(2)}) %collective-permute-start.15) | collective-permute-done | bytes 393248 | tf_op jit(solution)/shard_map/ppermute | solution.py:60
  556.1 5.1 all-to-all-start.3
  561.3 7.6 all-to-all-done.3
  568.9 7.4 collective-permute-start.24
  591.9 27.3 %reduce-scatter.5.cloned.1.call-done = bf16[48,1536]{1,0:T(8,128)(2,1)} async-done(((bf16[768,1536]{1,0:T(8,128)(2,1)}), bf16[48,1536]{1,0:T(8,128)(2,1)}) %reduce-scatter.5.cloned.1.call-update) | async-done | bytes 147472 | tf_op jit(solution)/shard_map/reduce_scatter | solution.py:218
  629.8 70.4 %reduce-scatter.11.cloned.1.call-done = bf16[48,3072]{1,0:T(8,128)(2,1)} async-done(((bf16[768,3072]{1,0:T(8,128)(2,1)}), bf16[48,3072]{1,0:T(8,128)(2,1)}) %reduce-scatter.11.cloned.1.call-update) | async-done | bytes 294928 | tf_op jit(solution)/shard_map/reduce_scatter | solution.py:218
  710.6 5.4 collective-permute-done.31
  717.2 64.0 %reduce-scatter.9.cloned.1.call-done = bf16[48,3072]{1,0:T(8,128)(2,1)} async-done(((bf16[768,3072]{1,0:T(8,128)(2,1)}), bf16[48,3072]{1,0:T(8,128)(2,1)}) %reduce-scatter.9.cloned.1.call-update) | async-done | bytes 294928 | tf_op jit(solution)/shard_map/reduce_scatter | solution.py:218
  786.9 4.7 collective-permute-done.27
  791.6 5.4 collective-permute-done.28
  (574 shorter events, 372.2 us)
Async XLA Ops:
  11.4 100.9 %all-to-all-start = ((bf16[16,8,128]{2,1,0:T(8,128)(2,1)}), bf16[16,8,128]{2,1,0:T(8,128)(2,1)S(1)}, u32[]{:S(2)}, u32[]{:S(2)}) async-start(bf16[16,8,128]{2,1,0:T(8,128)(2,1)} %broadcast_in_dim.34), calls=%async_computation | async-start | bytes 65536 | tf_op jit(solution)/shard_map/all_to_all | solution.py:133
  112.3 111.2 %all-to-all-start.1 = ((bf16[16,48,4608]{2,1,0:T(8,128)(2,1)}), bf16[16,48,4608]{2,1,0:T(8,128)(2,1)}, u32[]{:S(2)}, u32[]{:S(2)}) async-start(bf16[16,48,4608]{2,1,0:T(8,128)(2,1)} %bitcast.14), calls=%async_computation.1 | async-start | bytes 14155776 | tf_op jit(solution)/shard_map/all_to_all | solution.py:121
  119.7 120.5 %collective-permute-start.2 = (s32[2,128]{1,0:T(2,128)S(1)}, s32[2,128]{1,0:T(2,128)S(1)}, u32[]{:S(2)}, u32[]{:S(2)}) collective-permute-start(s32[2,128]{1,0:T(2,128)S(1)} %copy-done.72), channel_id=1, source_target_pairs={{0,4},{2,6},{1,5},{3,7},{8,12},{10,14},{9,13},{11,15},{16,20},{18,... | collective-permute-start | bytes 3080 | tf_op jit(solution)/shard_map/ppermute | solution.py:55
  124.8 115.4 %collective-permute-start.3 = (s32[2,128]{1,0:T(2,128)S(1)}, s32[2,128]{1,0:T(2,128)S(1)}, u32[]{:S(2)}, u32[]{:S(2)}) collective-permute-start(s32[2,128]{1,0:T(2,128)S(1)} %copy-done.72), channel_id=1, source_target_pairs={{0,2},{2,4},{4,6},{1,3},{3,5},{5,7},{8,10},{10,12},{12,14},{9,11},... | collective-permute-start | bytes 3080 | tf_op jit(solution)/shard_map/ppermute | solution.py:55
  223.5 106.8 %all-to-all-start.2 = ((bf16[16,48,4608]{2,1,0:T(8,128)(2,1)}), bf16[16,48,4608]{2,1,0:T(8,128)(2,1)}, u32[]{:S(2)}, u32[]{:S(2)}) async-start(bf16[16,48,4608]{2,1,0:T(8,128)(2,1)} %bitcast.413), calls=%async_computation.2 | async-start | bytes 14155776 | tf_op jit(solution)/shard_map/all_to_all | solution.py:121
  228.9 352.8 %reduce-scatter.7.cloned.1.call-start = ((), (), s32[]{:S(2)}) async-start(), calls=%async_computation.9 | async-start | bytes 2506752 | tf_op jit(solution)/shard_map/reduce_scatter | solution.py:218
  231.7 14.7 %collective-permute-start = (bf16[2,128,768]{2,1,0:T(8,128)(2,1)S(1)}, bf16[2,128,768]{2,1,0:T(8,128)(2,1)S(1)}, u32[]{:S(2)}, u32[]{:S(2)}) collective-permute-start(bf16[2,128,768]{2,1,0:T(8,128)(2,1)S(1)} %bitcast.432), channel_id=1, source_target_pairs={{0,4},{2,6},{1,5},{3,7},{8,12},{10,14},{9,13},{11,15},{16,20},{18,... | collective-permute-start | bytes 1179656 | tf_op jit(solution)/shard_map/ppermute | solution.py:55
  236.9 14.8 %collective-permute-start.1 = (bf16[2,128,768]{2,1,0:T(8,128)(2,1)S(1)}, bf16[2,128,768]{2,1,0:T(8,128)(2,1)}, u32[]{:S(2)}, u32[]{:S(2)}) collective-permute-start(bf16[2,128,768]{2,1,0:T(8,128)(2,1)S(1)} %bitcast.433), channel_id=1, source_target_pairs={{0,2},{2,4},{4,6},{1,3},{3,5},{5,7},{8,10},{10,12},{12,14},{9,11},... | collective-permute-start | bytes 1179656 | tf_op jit(solution)/shard_map/ppermute | solution.py:55
  333.6 15.0 %collective-permute-start.6 = (bf16[2,128,768]{2,1,0:T(8,128)(2,1)}, bf16[2,128,768]{2,1,0:T(8,128)(2,1)}, u32[]{:S(2)}, u32[]{:S(2)}) collective-permute-start(bf16[2,128,768]{2,1,0:T(8,128)(2,1)} %bitcast.34), channel_id=1, source_target_pairs={{0,4},{2,6},{1,5},{3,7},{8,12},{10,14},{9,13},{11,15},{16,20},{18,... | collective-permute-start | bytes 1179656 | tf_op jit(solution)/shard_map/ppermute | solution.py:55
  339.4 13.5 %collective-permute-start.7 = (bf16[2,128,768]{2,1,0:T(8,128)(2,1)}, bf16[2,128,768]{2,1,0:T(8,128)(2,1)}, u32[]{:S(2)}, u32[]{:S(2)}) collective-permute-start(bf16[2,128,768]{2,1,0:T(8,128)(2,1)} %bitcast.34), channel_id=1, source_target_pairs={{0,2},{2,4},{4,6},{1,3},{3,5},{5,7},{8,10},{10,12},{12,14},{9,11},... | collective-permute-start | bytes 1179656 | tf_op jit(solution)/shard_map/ppermute | solution.py:55
  425.3 14.5 %collective-permute-start.11 = (bf16[2,128,768]{2,1,0:T(8,128)(2,1)}, bf16[2,128,768]{2,1,0:T(8,128)(2,1)}, u32[]{:S(2)}, u32[]{:S(2)}) collective-permute-start(bf16[2,128,768]{2,1,0:T(8,128)(2,1)} %get-tuple-element.106), channel_id=1, source_target_pairs={{2,0},{4,2},{6,4},{3,1},{5,3},{7,5},{10,8},{12,10},{14,12},{11,9},... | collective-permute-start | bytes 1179656 | tf_op jit(solution)/shard_map/ppermute | solution.py:60
  426.8 16.2 %collective-permute-start.12 = (bf16[2,128,768]{2,1,0:T(8,128)(2,1)}, bf16[2,128,768]{2,1,0:T(8,128)(2,1)}, u32[]{:S(2)}, u32[]{:S(2)}) collective-permute-start(bf16[2,128,768]{2,1,0:T(8,128)(2,1)} %get-tuple-element.107), channel_id=1, source_target_pairs={{4,0},{6,2},{5,1},{7,3},{12,8},{14,10},{13,9},{15,11},{20,16},{22,... | collective-permute-start | bytes 1179656 | tf_op jit(solution)/shard_map/ppermute | solution.py:60
  462.1 157.1 %reduce-scatter.5.cloned.1.call-start = ((), (), s32[]{:S(2)}) async-start(), calls=%async_computation.8 | async-start | bytes 2506752 | tf_op jit(solution)/shard_map/reduce_scatter | solution.py:218
  486.7 19.5 %collective-permute-start.15 = (bf16[2,128,768]{2,1,0:T(8,128)(2,1)}, bf16[2,128,768]{2,1,0:T(8,128)(2,1)}, u32[]{:S(2)}, u32[]{:S(2)}) collective-permute-start(bf16[2,128,768]{2,1,0:T(8,128)(2,1)} %get-tuple-element.104), channel_id=1, source_target_pairs={{2,0},{4,2},{6,4},{3,1},{5,3},{7,5},{10,8},{12,10},{14,12},{11,9},... | collective-permute-start | bytes 1179656 | tf_op jit(solution)/shard_map/ppermute | solution.py:60
  488.0 21.1 %collective-permute-start.16 = (bf16[2,128,768]{2,1,0:T(8,128)(2,1)S(1)}, bf16[2,128,768]{2,1,0:T(8,128)(2,1)}, u32[]{:S(2)}, u32[]{:S(2)}) collective-permute-start(bf16[2,128,768]{2,1,0:T(8,128)(2,1)S(1)} %get-tuple-element.105), channel_id=1, source_target_pairs={{4,0},{6,2},{5,1},{7,3},{12,8},{14,10},{13,9},{15,11},{20,16},{22,... | collective-permute-start | bytes 1179656 | tf_op jit(solution)/shard_map/ppermute | solution.py:60
  514.6 185.6 %reduce-scatter.11.cloned.1.call-start = ((), (), s32[]{:S(2)}) async-start(), calls=%async_computation.11 | async-start | bytes 5013504 | tf_op jit(solution)/shard_map/reduce_scatter | solution.py:218
  522.0 259.1 %reduce-scatter.9.cloned.1.call-start = ((), (), s32[]{:S(2)}) async-start(), calls=%async_computation.10 | async-start | bytes 5013504 | tf_op jit(solution)/shard_map/reduce_scatter | solution.py:218
  556.1 12.8 %all-to-all-start.3 = ((f32[16,8,128]{2,1,0:T(8,128)}), f32[16,8,128]{2,1,0:T(8,128)S(1)}, u32[]{:S(2)}, u32[]{:S(2)}) async-start(f32[16,8,128]{2,1,0:T(8,128)} %bitcast.127), calls=%async_computation.5 | async-start | bytes 131072 | tf_op jit(solution)/shard_map/all_to_all | solution.py:319
  568.9 12.1 %collective-permute-start.24 = (f32[8,128]{1,0:T(8,128)S(1)}, f32[8,128]{1,0:T(8,128)S(1)}, u32[]{:S(2)}, u32[]{:S(2)}) collective-permute-start(f32[8,128]{1,0:T(8,128)S(1)} %reduce_sum.395), channel_id=1, source_target_pairs={{0,2},{2,4},{4,6},{6,0},{1,3},{3,5},{5,7},{7,1},{8,10},{10,12},{12... | collective-permute-start | bytes 12296 | tf_op jit(solution)/shard_map/ppermute | solution.py:67
  700.2 10.4 %collective-permute-start.30 = (bf16[48,3072]{1,0:T(8,128)(2,1)}, bf16[48,3072]{1,0:T(8,128)(2,1)S(1)}, u32[]{:S(2)}, u32[]{:S(2)}) collective-permute-start(bf16[48,3072]{1,0:T(8,128)(2,1)} %reduce-scatter.11.cloned.1.call-done), channel_id=1, source_target_pairs={{0,2},{2,4},{4,6},{6,0},{1,3},{3,5},{5,7},{7,1},{8,10},{10,12},{12... | collective-permute-start | bytes 884744 | tf_op jit(solution)/shard_map/ppermute | solution.py:67
  701.7 14.4 %collective-permute-start.31 = (bf16[48,3072]{1,0:T(8,128)(2,1)}, bf16[48,3072]{1,0:T(8,128)(2,1)S(1)}, u32[]{:S(2)}, u32[]{:S(2)}) collective-permute-start(bf16[48,3072]{1,0:T(8,128)(2,1)} %reduce-scatter.11.cloned.1.call-done), channel_id=1, source_target_pairs={{0,4},{2,6},{4,0},{6,2},{1,5},{3,7},{5,1},{7,3},{8,12},{10,14},{12... | collective-permute-start | bytes 884744 | tf_op jit(solution)/shard_map/ppermute | solution.py:67
  704.4 11.6 %collective-permute-start.32 = (bf16[48,3072]{1,0:T(8,128)(2,1)}, bf16[48,3072]{1,0:T(8,128)(2,1)S(1)}, u32[]{:S(2)}, u32[]{:S(2)}) collective-permute-start(bf16[48,3072]{1,0:T(8,128)(2,1)} %reduce-scatter.11.cloned.1.call-done), channel_id=1, source_target_pairs={{0,6},{2,0},{4,2},{6,4},{1,7},{3,1},{5,3},{7,5},{8,14},{10,8},{12,... | collective-permute-start | bytes 884744 | tf_op jit(solution)/shard_map/ppermute | solution.py:67
  782.7 14.4 %collective-permute-start.28 = (bf16[48,3072]{1,0:T(8,128)(2,1)}, bf16[48,3072]{1,0:T(8,128)(2,1)S(1)}, u32[]{:S(2)}, u32[]{:S(2)}) collective-permute-start(bf16[48,3072]{1,0:T(8,128)(2,1)} %reduce-scatter.9.cloned.1.call-done), channel_id=1, source_target_pairs={{0,4},{2,6},{4,0},{6,2},{1,5},{3,7},{5,1},{7,3},{8,12},{10,14},{12... | collective-permute-start | bytes 884744 | tf_op jit(solution)/shard_map/ppermute | solution.py:67
  785.4 11.6 %collective-permute-start.29 = (bf16[48,3072]{1,0:T(8,128)(2,1)}, bf16[48,3072]{1,0:T(8,128)(2,1)S(1)}, u32[]{:S(2)}, u32[]{:S(2)}) collective-permute-start(bf16[48,3072]{1,0:T(8,128)(2,1)} %reduce-scatter.9.cloned.1.call-done), channel_id=1, source_target_pairs={{0,6},{2,0},{4,2},{6,4},{1,7},{3,1},{5,3},{7,5},{8,14},{10,8},{12,... | collective-permute-start | bytes 884744 | tf_op jit(solution)/shard_map/ppermute | solution.py:67
  (93 other events, 1638.2 us)
Sparse Core Ops, SparseCore 0:
  462.2 79.3 reduce-scatter.6
  544.9 74.2 reduce-scatter.4
  622.5 77.6 reduce-scatter.10
  703.4 77.7 reduce-scatter.8
